TPU v7x, 512 devices: a whole 4x4x16 slice. The times are simulated.
512 devices in a mesh: tx: 8 (over x, core), ty: 16 (over z), tz: 4 (over y).
Axes of the slice: x: 4, y: 4, z: 16, core: 2. Of those that a mesh axis runs over, the one named last changes fastest.
Arguments:
- start_block: float32 [64, 1048576], P(None, ('tx', 'ty', 'tz'))
- weights: bfloat16 [8192, 6, 128, 128], P(('tx', 'ty', 'tz')), may hold values from 0 to 0.25, as said below
- neighbours: int32 [8192, 6], P(('tx', 'ty', 'tz')), may hold values from 0 to 123, as said below
- boundary: int32 [2048], P(('tx', 'ty', 'tz')), may hold values from 0 to 15, as said below
Outputs:
- basis: float32 [64, 1048576], P(None, ('tx', 'ty', 'tz'))
- rfactor: float32 [64, 64], replicated
Inputs may be any that keep to these rules, and one draw needn't show every extreme that they name: `neighbours`: slot 0 of block row b is b % 16; in the last of each device's 16 rows slot 1 is 123. `boundary`: each device's 4 entries are distinct, the last of them 16 - 1. For each block row b and point p, exactly 16 of the entries weights[b, s, q, p] over all slots s and rows q are nonzero, each positive.
All inputs are finite; a program needn't handle non-finite values.
Results may differ from a plain program's by a relative error of at most 0.00075.
Values may be sent and summed in bfloat16 or wider, within the bound.
No kernel may reach another device: no remote copies, remote signals or barrier semaphores. Data moves between devices by JAX's collectives and lax.ppermute only.
A program may use at most 64 MiB of HBM per device.

v0:
```python
import jax
import jax.numpy as jnp
from jax import lax
from jax.sharding import PartitionSpec as P


def extended(block, sides, width):
    for axis, dim in sides:
        count = lax.axis_size(axis)
        forward = [(i, i + 1) for i in range(count - 1)]
        backward = [(target, source) for source, target in forward]
        low = lax.ppermute(
            lax.slice_in_dim(block, block.shape[dim] - width, None, axis=dim), axis, forward
        )
        high = lax.ppermute(lax.slice_in_dim(block, 0, width, axis=dim), axis, backward)
        block = jnp.concatenate([low, block, high], axis=dim)
    return block


def take_edges(grid, boundary):
    return jnp.take(grid, boundary, axis=1)[:, None, None, None]


def boundary_halo(edge_part):
    return extended(edge_part, (("tx", 1), ("ty", 2), ("tz", 3)), 1)


def as_pool(haloed):
    return haloed.reshape(haloed.shape[0], -1, haloed.shape[-1])


def apply_operator(current, own_grid, far_grid, degree, weights, neighbours):
    pool_grid = jnp.concatenate([own_grid, far_grid], axis=1)
    picked = jnp.take(pool_grid, neighbours, axis=1)
    product = jnp.einsum("kisq,isqp->kip", picked, weights, preferred_element_type=jnp.float32)
    return current * (1.0 - degree * 0.125) + product.reshape(current.shape) * 0.125


def lower_factor(mixed):
    local_gram = jnp.dot(
        mixed, mixed.T, precision=lax.Precision.HIGHEST, preferred_element_type=jnp.float32
    )
    total = lax.psum(local_gram, ("tx", "ty", "tz"))
    return jnp.linalg.cholesky(total)


def solve_lower(lower, values):
    return lax.linalg.triangular_solve(lower, values, left_side=True, lower=True)


def per_device(start_block, weights, neighbours, boundary):
    width, points = start_block.shape
    block_size = weights.shape[-1]
    blocks = points // block_size
    devices = lax.axis_size("tx") * lax.axis_size("ty") * lax.axis_size("tz")
    root_scale = float(points * devices) ** 0.5
    degree = jnp.sum(weights, axis=(1, 2), dtype=jnp.float32).reshape(points)
    own_grid = start_block.astype(jnp.bfloat16).reshape(width, blocks, block_size)
    far_grid = as_pool(boundary_halo(take_edges(own_grid, boundary)))
    mixed = apply_operator(start_block, own_grid, far_grid, degree, weights, neighbours)
    lower = lower_factor(mixed)
    current = solve_lower(lower, mixed) * root_scale
    own_grid = current.astype(jnp.bfloat16).reshape(width, blocks, block_size)
    far_grid = as_pool(boundary_halo(take_edges(own_grid, boundary)))
    mixed = apply_operator(current, own_grid, far_grid, degree, weights, neighbours)
    lower = lower_factor(mixed)
    basis = solve_lower(lower, mixed) * root_scale
    return (basis, lower.T / root_scale)


def solution(mesh):
    placed = (
        P(None, ("tx", "ty", "tz")),
        P(("tx", "ty", "tz"), None, None, None),
        P(("tx", "ty", "tz"), None),
        P(("tx", "ty", "tz")),
    )
    return jax.shard_map(
        per_device,
        mesh=mesh,
        in_specs=placed,
        out_specs=(P(None, ("tx", "ty", "tz")), P()),
        check_vma=False,
    )
```

profile of v0, /device:TPU:1, one launch (start us, length us, event | category | flops | bytes accessed | tf_op | source)
XLA Modules:
  0.0 328.7 jit_solution(997474695390738293)
XLA Ops:
  2.0 1.1 copy_bitcast_fusion.1
  3.7 8.8 %collective-permute-start.1 = (bf16[64,1,1,1,4,128]{5,0,4,3,2,1:T(8,128)(2,1)S(1)}, bf16[64,1,1,1,4,128]{5,0,4,3,2,1:T(8,128)(2,1)S(1)}, u32[]{:S(2)}, u32[]{:S(2)}) collective-permute-start(bf16[64,1,1,1,4,128]{5,0,4,3,2,1:T(8,128)(2,1)S(1)} %select_bitcast_fusion.1), channel_id=1, source_target_pairs={{64,0},{128,64},{192,128},{256,192},{320,256},{384,320},{448,384},... | collective-permute-start | bytes 196616 | tf_op jit(solution)/shard_map/ppermute | solution.py:15
  12.5 1.9 collective-permute-start
  15.8 1.3 collective-permute-start.3
  17.1 4.0 %collective-permute-start.2 = (bf16[64,3,1,1,4,128]{5,0,4,3,2,1:T(8,128)(2,1)S(1)}, bf16[64,3,1,1,4,128]{5,0,4,3,2,1:T(8,128)(2,1)S(1)}, u32[]{:S(2)}, u32[]{:S(2)}) collective-permute-start(bf16[64,3,1,1,4,128]{5,0,4,3,2,1:T(8,128)(2,1)S(1)} %pad_maximum_fusion.6), channel_id=1, source_target_pairs={{0,4},{4,8},{8,12},{12,16},{16,20},{20,24},{24,28},{28,32},{32,36}... | collective-permute-start | bytes 589832 | tf_op jit(solution)/shard_map/ppermute | solution.py:12
  21.9 2.2 collective-permute-done.3
  25.0 1.3 collective-permute-start.5
  26.3 4.0 %collective-permute-start.4 = (bf16[64,3,3,1,4,128]{5,0,4,3,2,1:T(8,128)(2,1)S(1)}, bf16[64,3,3,1,4,128]{5,0,4,3,2,1:T(8,128)(2,1)S(1)}, u32[]{:S(2)}, u32[]{:S(2)}) collective-permute-start(bf16[64,3,3,1,4,128]{5,0,4,3,2,1:T(8,128)(2,1)S(1)} %pad_maximum_fusion.4), channel_id=1, source_target_pairs={{0,1},{1,2},{2,3},{4,5},{5,6},{6,7},{8,9},{9,10},{10,11},{12,13},{... | collective-permute-start | bytes 1769480 | tf_op jit(solution)/shard_map/ppermute | solution.py:12
  30.4 2.4 convert_reduce_fusion
  32.8 7.8 %collective-permute-done.5 = bf16[64,3,3,1,4,128]{5,0,4,3,2,1:T(8,128)(2,1)S(1)} collective-permute-done((bf16[64,3,3,1,4,128]{5,0,4,3,2,1:T(8,128)(2,1)S(1)}, bf16[64,3,3,1,4,128]{5,0,4,3,2,1:T(8,128)(2,1)S(1)}, u32[]{:S(2)}, u32[]{:S(2)}) %collective-permute-start.5) | collective-permute-done | bytes 589856 | tf_op jit(solution)/shard_map/ppermute | solution.py:15
  40.6 0.9 collective-permute-done.4
  41.9 2.0 gather_fusion.1
  43.9 3.2 fusion.23
  47.6 108.8 %psum.14 = f32[64,64]{0,1:T(8,128)S(1)} all-reduce(f32[64,64]{0,1:T(8,128)S(1)} %fusion.30), channel_id=1, replica_groups=mesh['tx'=8,'ty'=16,'tz'=4] {'tx','ty','tz'}, use_global_device_ids=true, to_apply=%region_1.4 | all-reduce | flops 4096 | bytes 32768 | tf_op jit(solution)/shard_map/psum | solution.py:43
  156.5 5.8 %cholesky.44 = f32[64,64]{1,0:T(8,128)S(1)} custom-call(f32[64,64]{1,0:T(8,128)S(1)} %fusion.36), custom_call_target="Cholesky" | custom-call | tf_op jit(solution)/shard_map/jit(cholesky)/cholesky | solution.py:44
  163.7 4.9 %custom-call.6 = f32[1,64,64]{1,2,0:T(8,128)S(1)} custom-call(f32[1,64,64]{2,1,0:T(8,128)S(1)} %fusion.32), custom_call_target="InvertDiagBlocksLowerTriangular" | custom-call | tf_op jit(solution)/shard_map/triangular_solve/custom-call.0 | solution.py:48
  170.0 2.6 collective-permute-start.7
  172.6 3.0 collective-permute-start.6
  175.6 1.3 collective-permute-done.6
  176.9 1.3 collective-permute-start.9
  178.2 4.3 %collective-permute-start.8 = (bf16[64,3,1,1,4,128]{5,0,4,3,2,1:T(8,128)(2,1)S(1)}, bf16[64,3,1,1,4,128]{5,0,4,3,2,1:T(8,128)(2,1)S(1)}, u32[]{:S(2)}, u32[]{:S(2)}) collective-permute-start(bf16[64,3,1,1,4,128]{5,0,4,3,2,1:T(8,128)(2,1)S(1)} %pad_maximum_fusion.7), channel_id=1, source_target_pairs={{0,4},{4,8},{8,12},{12,16},{16,20},{20,24},{24,28},{28,32},{32,36}... | collective-permute-start | bytes 589832 | tf_op jit(solution)/shard_map/ppermute | solution.py:12
  182.4 2.4 collective-permute-done.9
  184.9 1.8 collective-permute-done.8
  186.7 1.3 collective-permute-start.11
  188.0 4.0 %collective-permute-start.10 = (bf16[64,3,3,1,4,128]{5,0,4,3,2,1:T(8,128)(2,1)S(1)}, bf16[64,3,3,1,4,128]{5,0,4,3,2,1:T(8,128)(2,1)S(1)}, u32[]{:S(2)}, u32[]{:S(2)}) collective-permute-start(bf16[64,3,3,1,4,128]{5,0,4,3,2,1:T(8,128)(2,1)S(1)} %pad_maximum_fusion.5), channel_id=1, source_target_pairs={{0,1},{1,2},{2,3},{4,5},{5,6},{6,7},{8,9},{9,10},{10,11},{12,13},{... | collective-permute-start | bytes 1769480 | tf_op jit(solution)/shard_map/ppermute | solution.py:12
  192.0 11.6 %collective-permute-done.11 = bf16[64,3,3,1,4,128]{5,0,4,3,2,1:T(8,128)(2,1)S(1)} collective-permute-done((bf16[64,3,3,1,4,128]{5,0,4,3,2,1:T(8,128)(2,1)S(1)}, bf16[64,3,3,1,4,128]{5,0,4,3,2,1:T(8,128)(2,1)S(1)}, u32[]{:S(2)}, u32[]{:S(2)}) %collective-permute-start.11) | collective-permute-done | bytes 589856 | tf_op jit(solution)/shard_map/ppermute | solution.py:15
  204.9 2.0 gather_fusion.3
  206.9 3.1 fusion.17
  210.5 103.8 %psum.15 = f32[64,64]{0,1:T(8,128)S(1)} all-reduce(f32[64,64]{0,1:T(8,128)S(1)} %fusion.31), channel_id=1, replica_groups=mesh['tx'=8,'ty'=16,'tz'=4] {'tx','ty','tz'}, use_global_device_ids=true, to_apply=%region_4.9 | all-reduce | flops 4096 | bytes 32768 | tf_op jit(solution)/shard_map/psum | solution.py:43
  314.5 5.8 %cholesky.55 = f32[64,64]{1,0:T(8,128)S(1)} custom-call(f32[64,64]{1,0:T(8,128)S(1)} %fusion.34), custom_call_target="Cholesky" | custom-call | tf_op jit(solution)/shard_map/jit(cholesky)/cholesky | solution.py:44
  322.4 4.9 %custom-call.7 = f32[1,64,64]{1,2,0:T(8,128)S(1)} custom-call(f32[1,64,64]{2,1,0:T(8,128)S(1)} %get-tuple-element.13), custom_call_target="InvertDiagBlocksLowerTriangular" | custom-call | tf_op jit(solution)/shard_map/triangular_solve/custom-call.0 | solution.py:48
  327.3 1.4 convolution_multiply_fusion
  (45 shorter events, 12.9 us)
Async XLA Ops:
  3.7 11.5 %collective-permute-start.1 = (bf16[64,1,1,1,4,128]{5,0,4,3,2,1:T(8,128)(2,1)S(1)}, bf16[64,1,1,1,4,128]{5,0,4,3,2,1:T(8,128)(2,1)S(1)}, u32[]{:S(2)}, u32[]{:S(2)}) collective-permute-start(bf16[64,1,1,1,4,128]{5,0,4,3,2,1:T(8,128)(2,1)S(1)} %select_bitcast_fusion.1), channel_id=1, source_target_pairs={{64,0},{128,64},{192,128},{256,192},{320,256},{384,320},{448,384},... | collective-permute-start | bytes 196616 | tf_op jit(solution)/shard_map/ppermute | solution.py:15
  12.5 3.2 collective-permute-start
  15.8 8.3 %collective-permute-start.3 = (bf16[64,3,1,1,4,128]{5,0,4,3,2,1:T(8,128)(2,1)S(1)}, bf16[64,3,1,1,4,128]{5,0,4,3,2,1:T(8,128)(2,1)S(1)}, u32[]{:S(2)}, u32[]{:S(2)}) collective-permute-start(bf16[64,3,1,1,4,128]{5,0,4,3,2,1:T(8,128)(2,1)S(1)} %pad_maximum_fusion.6), channel_id=1, source_target_pairs={{4,0},{8,4},{12,8},{16,12},{20,16},{24,20},{28,24},{32,28},{36,32}... | collective-permute-start | bytes 589832 | tf_op jit(solution)/shard_map/ppermute | solution.py:15
  17.1 7.9 %collective-permute-start.2 = (bf16[64,3,1,1,4,128]{5,0,4,3,2,1:T(8,128)(2,1)S(1)}, bf16[64,3,1,1,4,128]{5,0,4,3,2,1:T(8,128)(2,1)S(1)}, u32[]{:S(2)}, u32[]{:S(2)}) collective-permute-start(bf16[64,3,1,1,4,128]{5,0,4,3,2,1:T(8,128)(2,1)S(1)} %pad_maximum_fusion.6), channel_id=1, source_target_pairs={{0,4},{4,8},{8,12},{12,16},{16,20},{20,24},{24,28},{28,32},{32,36}... | collective-permute-start | bytes 589832 | tf_op jit(solution)/shard_map/ppermute | solution.py:12
  25.0 15.5 %collective-permute-start.5 = (bf16[64,3,3,1,4,128]{5,0,4,3,2,1:T(8,128)(2,1)S(1)}, bf16[64,3,3,1,4,128]{5,0,4,3,2,1:T(8,128)(2,1)S(1)}, u32[]{:S(2)}, u32[]{:S(2)}) collective-permute-start(bf16[64,3,3,1,4,128]{5,0,4,3,2,1:T(8,128)(2,1)S(1)} %pad_maximum_fusion.4), channel_id=1, source_target_pairs={{1,0},{2,1},{3,2},{5,4},{6,5},{7,6},{9,8},{10,9},{11,10},{13,12},{... | collective-permute-start | bytes 1769480 | tf_op jit(solution)/shard_map/ppermute | solution.py:15
  26.3 15.1 %collective-permute-start.4 = (bf16[64,3,3,1,4,128]{5,0,4,3,2,1:T(8,128)(2,1)S(1)}, bf16[64,3,3,1,4,128]{5,0,4,3,2,1:T(8,128)(2,1)S(1)}, u32[]{:S(2)}, u32[]{:S(2)}) collective-permute-start(bf16[64,3,3,1,4,128]{5,0,4,3,2,1:T(8,128)(2,1)S(1)} %pad_maximum_fusion.4), channel_id=1, source_target_pairs={{0,1},{1,2},{2,3},{4,5},{5,6},{6,7},{8,9},{9,10},{10,11},{12,13},{... | collective-permute-start | bytes 1769480 | tf_op jit(solution)/shard_map/ppermute | solution.py:12
  43.9 3.2 copy-start
  170.0 5.6 %collective-permute-start.7 = (bf16[64,1,1,1,4,128]{5,0,4,3,2,1:T(8,128)(2,1)S(1)}, bf16[64,1,1,1,4,128]{5,0,4,3,2,1:T(8,128)(2,1)S(1)}, u32[]{:S(2)}, u32[]{:S(2)}) collective-permute-start(bf16[64,1,1,1,4,128]{5,0,4,3,2,1:T(8,128)(2,1)S(1)} %select_bitcast_fusion), channel_id=1, source_target_pairs={{64,0},{128,64},{192,128},{256,192},{320,256},{384,320},{448,384},... | collective-permute-start | bytes 196616 | tf_op jit(solution)/shard_map/ppermute | solution.py:15
  172.6 4.3 %collective-permute-start.6 = (bf16[64,1,1,1,4,128]{5,0,4,3,2,1:T(8,128)(2,1)S(1)}, bf16[64,1,1,1,4,128]{5,0,4,3,2,1:T(8,128)(2,1)S(1)}, u32[]{:S(2)}, u32[]{:S(2)}) collective-permute-start(bf16[64,1,1,1,4,128]{5,0,4,3,2,1:T(8,128)(2,1)S(1)} %select_bitcast_fusion), channel_id=1, source_target_pairs={{0,64},{64,128},{128,192},{192,256},{256,320},{320,384},{384,448},... | collective-permute-start | bytes 196616 | tf_op jit(solution)/shard_map/ppermute | solution.py:12
  176.9 8.0 %collective-permute-start.9 = (bf16[64,3,1,1,4,128]{5,0,4,3,2,1:T(8,128)(2,1)S(1)}, bf16[64,3,1,1,4,128]{5,0,4,3,2,1:T(8,128)(2,1)S(1)}, u32[]{:S(2)}, u32[]{:S(2)}) collective-permute-start(bf16[64,3,1,1,4,128]{5,0,4,3,2,1:T(8,128)(2,1)S(1)} %pad_maximum_fusion.7), channel_id=1, source_target_pairs={{4,0},{8,4},{12,8},{16,12},{20,16},{24,20},{28,24},{32,28},{36,32}... | collective-permute-start | bytes 589832 | tf_op jit(solution)/shard_map/ppermute | solution.py:15
  178.2 8.4 %collective-permute-start.8 = (bf16[64,3,1,1,4,128]{5,0,4,3,2,1:T(8,128)(2,1)S(1)}, bf16[64,3,1,1,4,128]{5,0,4,3,2,1:T(8,128)(2,1)S(1)}, u32[]{:S(2)}, u32[]{:S(2)}) collective-permute-start(bf16[64,3,1,1,4,128]{5,0,4,3,2,1:T(8,128)(2,1)S(1)} %pad_maximum_fusion.7), channel_id=1, source_target_pairs={{0,4},{4,8},{8,12},{12,16},{16,20},{20,24},{24,28},{28,32},{32,36}... | collective-permute-start | bytes 589832 | tf_op jit(solution)/shard_map/ppermute | solution.py:12
  186.7 16.9 %collective-permute-start.11 = (bf16[64,3,3,1,4,128]{5,0,4,3,2,1:T(8,128)(2,1)S(1)}, bf16[64,3,3,1,4,128]{5,0,4,3,2,1:T(8,128)(2,1)S(1)}, u32[]{:S(2)}, u32[]{:S(2)}) collective-permute-start(bf16[64,3,3,1,4,128]{5,0,4,3,2,1:T(8,128)(2,1)S(1)} %pad_maximum_fusion.5), channel_id=1, source_target_pairs={{1,0},{2,1},{3,2},{5,4},{6,5},{7,6},{9,8},{10,9},{11,10},{13,12},{... | collective-permute-start | bytes 1769480 | tf_op jit(solution)/shard_map/ppermute | solution.py:15
  188.0 16.5 %collective-permute-start.10 = (bf16[64,3,3,1,4,128]{5,0,4,3,2,1:T(8,128)(2,1)S(1)}, bf16[64,3,3,1,4,128]{5,0,4,3,2,1:T(8,128)(2,1)S(1)}, u32[]{:S(2)}, u32[]{:S(2)}) collective-permute-start(bf16[64,3,3,1,4,128]{5,0,4,3,2,1:T(8,128)(2,1)S(1)} %pad_maximum_fusion.5), channel_id=1, source_target_pairs={{0,1},{1,2},{2,3},{4,5},{5,6},{6,7},{8,9},{9,10},{10,11},{12,13},{... | collective-permute-start | bytes 1769480 | tf_op jit(solution)/shard_map/ppermute | solution.py:12
where the time goes:
time: 330 us; the launch traced here: 329 us
  blocking collectives  213 us (65%)
  starting transfers between devices  37.7 us (11%)
  other arithmetic  31.6 us (10%)
  waiting for transfers between devices  30.1 us (9%)
  matrix products  9.49 us (3%)
  local copies, waits for them, and re-layouts  6.16 us (2%)
    psum x2, blocking collectives, lower_factor(): total = lax.psum(local_gram, ('tx', 'ty', 'tz'))  213 us
    ppermute x6, waiting for transfers between devices, extended(): lax.ppermute(lax.slice_in_dim(block, 0, width, axis=dim), axis, backward)  23.9 us
    ppermute x6, starting transfers between devices, extended(): lax.ppermute(lax.slice_in_dim(block, block.shape[dim] - width, None, axis...  21.2 us
    ppermute x6, starting transfers between devices, extended(): lax.ppermute(lax.slice_in_dim(block, 0, width, axis=dim), axis, backward)  16.5 us
    another operation x6, other arithmetic, lower_factor(): return jnp.linalg.cholesky(total)  13 us
    another operation x3, other arithmetic, solve_lower(): lax.linalg.triangular_solve(lower, values, left_side=True, lower=True)  10.4 us
  transfers between devices with their start and end apart: 12, of which 10 were waited for; matrix products, arithmetic and copies ran while one was open for 1% of the time, Pallas kernels for 0%

commit v1 on v0

--- a/solution.py
+++ b/solution.py
@@ -40,7 +40,8 @@
     local_gram = jnp.dot(
         mixed, mixed.T, precision=lax.Precision.HIGHEST, preferred_element_type=jnp.float32
     )
-    total = lax.psum(local_gram, ("tx", "ty", "tz"))
+    parts = lax.all_gather(local_gram, ("tx", "ty", "tz"))
+    total = jnp.sum(parts, axis=0)
     return jnp.linalg.cholesky(total)
 
 

time: 330 us -> 588 us (1.78)
  waiting for transfers between devices: 30.1 us -> 473 us
  blocking collectives: 213 us -> 0 us
  other arithmetic: 31.6 us -> 45.5 us
  between operations: 0.93 us -> 14.3 us
    all_gather x0 -> x2, waiting for transfers between devices: none -> 443 us  [lower_factor(): parts = lax.all_gather(local_gram, ('tx', 'ty', 'tz'))]
    psum x2 -> x0, blocking collectives: 213 us -> none  [lower_factor(): total = lax.psum(local_gram, ('tx', 'ty', 'tz'))]
    reduce_sum x0 -> x2, other arithmetic: none -> 13.9 us  [lower_factor(): total = jnp.sum(parts, axis=0)]
  transfers between devices with their start and end apart: 12 -> 14, of which waited for: 10 -> 12; matrix products, arithmetic and copies ran while one was open for 1% -> 1% of each run, Pallas kernels for 0% -> 0%
where the time goes in v1:
time: 588 us; the launch traced here: 587 us
  waiting for transfers between devices  473 us (80%)
  other arithmetic  45.5 us (8%)
  starting transfers between devices  37.7 us (6%)
  between operations  14.3 us (2%)
  matrix products  10.7 us (2%)
  local copies, waits for them, and re-layouts  6.16 us (1%)
    all_gather x2, waiting for transfers between devices, lower_factor(): parts = lax.all_gather(local_gram, ('tx', 'ty', 'tz'))  443 us
    ppermute x6, waiting for transfers between devices, extended(): lax.ppermute(lax.slice_in_dim(block, 0, width, axis=dim), axis, backward)  23.7 us
    ppermute x6, starting transfers between devices, extended(): lax.ppermute(lax.slice_in_dim(block, block.shape[dim] - width, None, axis...  21.6 us
    ppermute x6, starting transfers between devices, extended(): lax.ppermute(lax.slice_in_dim(block, 0, width, axis=dim), axis, backward)  16.1 us
    reduce_sum x2, other arithmetic, lower_factor(): total = jnp.sum(parts, axis=0)  13.9 us
    another operation x6, other arithmetic, lower_factor(): return jnp.linalg.cholesky(total)  13 us
  transfers between devices with their start and end apart: 14, of which 12 were waited for; matrix products, arithmetic and copies ran while one was open for 1% of the time, Pallas kernels for 0%

profile of v1, /device:TPU:1, one launch (start us, length us, event | category | flops | bytes accessed | tf_op | source)
XLA Modules:
  0.0 587.4 jit_solution(13456410168277262901)
XLA Ops:
  10.3 8.8 %collective-permute-start.1 = (bf16[64,1,1,1,4,128]{5,0,4,3,2,1:T(8,128)(2,1)S(1)}, bf16[64,1,1,1,4,128]{5,0,4,3,2,1:T(8,128)(2,1)S(1)}, u32[]{:S(2)}, u32[]{:S(2)}) collective-permute-start(bf16[64,1,1,1,4,128]{5,0,4,3,2,1:T(8,128)(2,1)S(1)} %select_bitcast_fusion.1), channel_id=1, source_target_pairs={{64,0},{128,64},{192,128},{256,192},{320,256},{384,320},{448,384},... | collective-permute-start | bytes 196616 | tf_op jit(solution)/shard_map/ppermute | solution.py:15
  19.1 1.9 collective-permute-start
  22.3 1.3 collective-permute-start.3
  23.6 4.0 collective-permute-start.2
  28.5 2.2 collective-permute-done.3
  31.6 1.3 collective-permute-start.5
  32.9 4.0 collective-permute-start.4
  37.0 2.4 convert_reduce_fusion
  39.4 7.8 %collective-permute-done.5 = bf16[64,3,3,1,4,128]{5,0,4,3,2,1:T(8,128)(2,1)S(1)} collective-permute-done((bf16[64,3,3,1,4,128]{5,0,4,3,2,1:T(8,128)(2,1)S(1)}, bf16[64,3,3,1,4,128]{5,0,4,3,2,1:T(8,128)(2,1)S(1)}, u32[]{:S(2)}, u32[]{:S(2)}) %collective-permute-start.5) | collective-permute-done | bytes 589856 | tf_op jit(solution)/shard_map/ppermute | solution.py:15
  48.5 2.0 gather_fusion.1
  50.4 3.2 fusion.23
  54.9 224.1 %all-gather.5.cloned.1.call-done = f32[32768,64]{1,0:T(8,128)} async-done(((f32[64,64]{1,0:T(8,128)}), f32[32768,64]{1,0:T(8,128)}) %all-gather.5.cloned.1.call-update) | async-done | bytes 8388624 | tf_op jit(solution)/shard_map/all_gather | solution.py:43
  278.9 6.9 %reduce_sum.28 = f32[64,64]{1,0:T(8,128)S(1)} reduce(f32[512,64,64]{2,1,0:T(8,128)} %bitcast.96, f32[]{:T(128)} %constant.57.clone.1), dimensions={0}, to_apply=%region_1.4 | reduce | flops 2093056 | bytes 8404996 | tf_op jit(solution)/shard_map/reduce_sum | solution.py:44
  286.0 5.8 cholesky.44
  293.2 4.9 custom-call.6
  299.4 2.1 collective-permute-start.7
  301.6 3.4 collective-permute-start.6
  305.0 1.3 collective-permute-done.6
  306.3 1.3 collective-permute-start.9
  307.6 4.0 collective-permute-start.8
  311.6 2.2 collective-permute-done.9
  313.9 1.8 collective-permute-done.8
  315.7 1.3 collective-permute-start.11
  317.0 4.2 collective-permute-start.10
  321.2 11.5 %collective-permute-done.11 = bf16[64,3,3,1,4,128]{5,0,4,3,2,1:T(8,128)(2,1)S(1)} collective-permute-done((bf16[64,3,3,1,4,128]{5,0,4,3,2,1:T(8,128)(2,1)S(1)}, bf16[64,3,3,1,4,128]{5,0,4,3,2,1:T(8,128)(2,1)S(1)}, u32[]{:S(2)}, u32[]{:S(2)}) %collective-permute-start.11) | collective-permute-done | bytes 589856 | tf_op jit(solution)/shard_map/ppermute | solution.py:15
  334.2 2.0 gather_fusion.3
  336.1 3.1 fusion.17
  340.4 218.9 %all-gather.7.cloned.1.call-done = f32[32768,64]{1,0:T(8,128)} async-done(((f32[64,64]{1,0:T(8,128)}), f32[32768,64]{1,0:T(8,128)}) %all-gather.7.cloned.1.call-update) | async-done | bytes 8388624 | tf_op jit(solution)/shard_map/all_gather | solution.py:43
  559.3 6.9 %reduce_sum.29 = f32[64,64]{1,0:T(8,128)S(1)} reduce(f32[512,64,64]{2,1,0:T(8,128)} %bitcast.97, f32[]{:T(128)} %constant.57.clone.1), dimensions={0}, to_apply=%region_4.9 | reduce | flops 2093056 | bytes 8404996 | tf_op jit(solution)/shard_map/reduce_sum | solution.py:44
  566.3 5.8 cholesky.55
  574.2 4.9 custom-call.7
  579.1 1.4 convolution_multiply_fusion
  (51 shorter events, 16.4 us)
Async XLA Ops:
  7.2 271.8 %all-gather.5.cloned.1.call-start = ((), (), s32[]{:S(2)}) async-start(), calls=%async_computation | async-start | bytes 16809984 | tf_op jit(solution)/shard_map/all_gather | solution.py:43
  10.3 11.5 %collective-permute-start.1 = (bf16[64,1,1,1,4,128]{5,0,4,3,2,1:T(8,128)(2,1)S(1)}, bf16[64,1,1,1,4,128]{5,0,4,3,2,1:T(8,128)(2,1)S(1)}, u32[]{:S(2)}, u32[]{:S(2)}) collective-permute-start(bf16[64,1,1,1,4,128]{5,0,4,3,2,1:T(8,128)(2,1)S(1)} %select_bitcast_fusion.1), channel_id=1, source_target_pairs={{64,0},{128,64},{192,128},{256,192},{320,256},{384,320},{448,384},... | collective-permute-start | bytes 196616 | tf_op jit(solution)/shard_map/ppermute | solution.py:15
  19.1 3.2 collective-permute-start
  22.3 8.3 %collective-permute-start.3 = (bf16[64,3,1,1,4,128]{5,0,4,3,2,1:T(8,128)(2,1)S(1)}, bf16[64,3,1,1,4,128]{5,0,4,3,2,1:T(8,128)(2,1)S(1)}, u32[]{:S(2)}, u32[]{:S(2)}) collective-permute-start(bf16[64,3,1,1,4,128]{5,0,4,3,2,1:T(8,128)(2,1)S(1)} %pad_maximum_fusion.6), channel_id=1, source_target_pairs={{4,0},{8,4},{12,8},{16,12},{20,16},{24,20},{28,24},{32,28},{36,32}... | collective-permute-start | bytes 589832 | tf_op jit(solution)/shard_map/ppermute | solution.py:15
  23.6 7.9 %collective-permute-start.2 = (bf16[64,3,1,1,4,128]{5,0,4,3,2,1:T(8,128)(2,1)S(1)}, bf16[64,3,1,1,4,128]{5,0,4,3,2,1:T(8,128)(2,1)S(1)}, u32[]{:S(2)}, u32[]{:S(2)}) collective-permute-start(bf16[64,3,1,1,4,128]{5,0,4,3,2,1:T(8,128)(2,1)S(1)} %pad_maximum_fusion.6), channel_id=1, source_target_pairs={{0,4},{4,8},{8,12},{12,16},{16,20},{20,24},{24,28},{28,32},{32,36}... | collective-permute-start | bytes 589832 | tf_op jit(solution)/shard_map/ppermute | solution.py:12
  31.6 15.5 %collective-permute-start.5 = (bf16[64,3,3,1,4,128]{5,0,4,3,2,1:T(8,128)(2,1)S(1)}, bf16[64,3,3,1,4,128]{5,0,4,3,2,1:T(8,128)(2,1)S(1)}, u32[]{:S(2)}, u32[]{:S(2)}) collective-permute-start(bf16[64,3,3,1,4,128]{5,0,4,3,2,1:T(8,128)(2,1)S(1)} %pad_maximum_fusion.4), channel_id=1, source_target_pairs={{1,0},{2,1},{3,2},{5,4},{6,5},{7,6},{9,8},{10,9},{11,10},{13,12},{... | collective-permute-start | bytes 1769480 | tf_op jit(solution)/shard_map/ppermute | solution.py:15
  32.9 15.1 %collective-permute-start.4 = (bf16[64,3,3,1,4,128]{5,0,4,3,2,1:T(8,128)(2,1)S(1)}, bf16[64,3,3,1,4,128]{5,0,4,3,2,1:T(8,128)(2,1)S(1)}, u32[]{:S(2)}, u32[]{:S(2)}) collective-permute-start(bf16[64,3,3,1,4,128]{5,0,4,3,2,1:T(8,128)(2,1)S(1)} %pad_maximum_fusion.4), channel_id=1, source_target_pairs={{0,1},{1,2},{2,3},{4,5},{5,6},{6,7},{8,9},{9,10},{10,11},{12,13},{... | collective-permute-start | bytes 1769480 | tf_op jit(solution)/shard_map/ppermute | solution.py:12
  50.4 3.2 copy-start
  54.8 504.5 %all-gather.7.cloned.1.call-start = ((), (), s32[]{:S(2)}) async-start(), calls=%async_computation.1 | async-start | bytes 16809984 | tf_op jit(solution)/shard_map/all_gather | solution.py:43
  299.4 5.6 collective-permute-start.7
  301.6 4.7 collective-permute-start.6
  306.3 7.6 %collective-permute-start.9 = (bf16[64,3,1,1,4,128]{5,0,4,3,2,1:T(8,128)(2,1)S(1)}, bf16[64,3,1,1,4,128]{5,0,4,3,2,1:T(8,128)(2,1)S(1)}, u32[]{:S(2)}, u32[]{:S(2)}) collective-permute-start(bf16[64,3,1,1,4,128]{5,0,4,3,2,1:T(8,128)(2,1)S(1)} %pad_maximum_fusion.7), channel_id=1, source_target_pairs={{4,0},{8,4},{12,8},{16,12},{20,16},{24,20},{28,24},{32,28},{36,32}... | collective-permute-start | bytes 589832 | tf_op jit(solution)/shard_map/ppermute | solution.py:15
  307.6 8.0 %collective-permute-start.8 = (bf16[64,3,1,1,4,128]{5,0,4,3,2,1:T(8,128)(2,1)S(1)}, bf16[64,3,1,1,4,128]{5,0,4,3,2,1:T(8,128)(2,1)S(1)}, u32[]{:S(2)}, u32[]{:S(2)}) collective-permute-start(bf16[64,3,1,1,4,128]{5,0,4,3,2,1:T(8,128)(2,1)S(1)} %pad_maximum_fusion.7), channel_id=1, source_target_pairs={{0,4},{4,8},{8,12},{12,16},{16,20},{20,24},{24,28},{28,32},{32,36}... | collective-permute-start | bytes 589832 | tf_op jit(solution)/shard_map/ppermute | solution.py:12
  315.7 17.0 %collective-permute-start.11 = (bf16[64,3,3,1,4,128]{5,0,4,3,2,1:T(8,128)(2,1)S(1)}, bf16[64,3,3,1,4,128]{5,0,4,3,2,1:T(8,128)(2,1)S(1)}, u32[]{:S(2)}, u32[]{:S(2)}) collective-permute-start(bf16[64,3,3,1,4,128]{5,0,4,3,2,1:T(8,128)(2,1)S(1)} %pad_maximum_fusion.5), channel_id=1, source_target_pairs={{1,0},{2,1},{3,2},{5,4},{6,5},{7,6},{9,8},{10,9},{11,10},{13,12},{... | collective-permute-start | bytes 1769480 | tf_op jit(solution)/shard_map/ppermute | solution.py:15
  317.0 16.7 %collective-permute-start.10 = (bf16[64,3,3,1,4,128]{5,0,4,3,2,1:T(8,128)(2,1)S(1)}, bf16[64,3,3,1,4,128]{5,0,4,3,2,1:T(8,128)(2,1)S(1)}, u32[]{:S(2)}, u32[]{:S(2)}) collective-permute-start(bf16[64,3,3,1,4,128]{5,0,4,3,2,1:T(8,128)(2,1)S(1)} %pad_maximum_fusion.5), channel_id=1, source_target_pairs={{0,1},{1,2},{2,3},{4,5},{5,6},{6,7},{8,9},{9,10},{10,11},{12,13},{... | collective-permute-start | bytes 1769480 | tf_op jit(solution)/shard_map/ppermute | solution.py:12
Sparse Core Ops, SparseCore 0:
  55.0 223.9 all-gather.4
  340.5 218.7 all-gather.6
